TPU v7x, 256 devices: a whole 4x4x8 slice. The times are simulated.
256 devices in a mesh: sec: 2 (over core), row: 4 (over x), col: 32 (over z, y).
Axes of the slice: x: 4, y: 4, z: 8, core: 2. Of those that a mesh axis runs over, the one named last changes fastest.
Arguments:
- leaf_rhs: bfloat16 [2, 4, 1, 32, 128, 256], P('sec', 'row', None, 'col'), may hold values from -6 to 6
- sep_rhs: bfloat16 [2, 4, 32, 128, 256], P('sec', 'row', 'col'), may hold values from -6 to 6
- top_rhs: bfloat16 [4, 32, 128, 256], P('row', 'col'), may hold values from -6 to 6
- leaf_inv: float32 [2, 4, 1, 32, 128, 128], P('sec', 'row', None, 'col'), may hold values from -1 to 3, as said below
- sep_inv: float32 [2, 4, 32, 128, 128], P('sec', 'row', 'col'), may hold values from -1 to 3, as said below
- top_inv: float32 [4, 32, 128, 128], P('row', 'col'), may hold values from -1 to 3, as said below
- sep_leaf: bfloat16 [2, 4, 32, 128, 4, 1, 32, 128], P('sec', 'row', None, None, None, None, 'col'), may hold values from -0.0625 to 0.0625
- top_leaf: bfloat16 [2, 4, 32, 128, 4, 1, 32, 128], P('sec', 'row', None, None, None, None, 'col'), may hold values from -0.046875 to 0.046875
- top_sep: bfloat16 [2, 4, 32, 128, 4, 32, 128], P('sec', 'row', None, None, None, 'col'), may hold values from -0.046875 to 0.046875
- sep_leaf_mask: int32 [2, 4, 32, 4, 1, 32], P('sec', 'row', None, None, None, 'col'), may hold values 0 or 1
- top_leaf_mask: int32 [2, 4, 32, 4, 1, 32], P('sec', 'row', None, None, None, 'col'), may hold values 0 or 1
- top_sep_mask: int32 [2, 4, 32, 4, 32], P('sec', 'row', None, None, 'col'), may hold values 0 or 1
Outputs:
- leaf_x: float32 [2, 4, 1, 32, 128, 256], P('sec', 'row', None, 'col')
- sep_x: float32 [2, 4, 32, 128, 256], P('sec', 'row', 'col')
- top_x: float32 [4, 32, 128, 256], P('row', 'col')
Inputs may be any that keep to these rules, and one draw needn't show every extreme that they name: `leaf_inv`: every 128 x 128 block is lower triangular with positive diagonal. `sep_inv`: every 128 x 128 block is lower triangular with positive diagonal. `top_inv`: every 128 x 128 block is lower triangular with positive diagonal.
All inputs are finite; a program needn't handle non-finite values. No bound on the sum of `sep_leaf_mask` or of `top_leaf_mask` or of `top_sep_mask` on one device may be relied on, other than what follows from the above.
Results may differ from a plain program's by a relative error of at most 0.0036.
Values may be sent and summed in bfloat16 or wider, within the bound.
A program may use at most 128 MiB of HBM per device.

v0:
```python
import jax
import jax.numpy as jnp
from jax import lax
from jax.sharding import PartitionSpec as P


def lower_apply(inverse, right_side):
    return jnp.einsum("...ab,...bn->...an", inverse, right_side, precision=lax.Precision.HIGHEST)


def upper_apply(inverse, right_side):
    return jnp.einsum("...ba,...bn->...an", inverse, right_side, precision=lax.Precision.HIGHEST)


def mask_tiles(tile_set, pattern):
    return tile_set * pattern.astype(jnp.bfloat16)[:, None, :, :, None]


def spread_down(values, update, totals):
    return update(totals, lax.all_gather(values, "row", axis=0, tiled=True), jnp.int32(0))


def reduce_row(partial_value, rhs_cols):
    col_count = lax.axis_size("col")
    summed = lax.psum_scatter(
        partial_value.reshape(col_count, partial_value.shape[0] // col_count, rhs_cols),
        "col",
        scatter_dimension=0,
        tiled=True,
    )
    return summed.reshape(summed.shape[1], rhs_cols)


def add_sections(partial_value):
    return lax.psum(partial_value, "sec")


def spread_across(values):
    return lax.all_gather(values[None], "col", axis=0, tiled=True)


def collect_up(term_fn, row_span):
    return lax.psum_scatter(
        term_fn(jnp.int32(0), row_span * lax.axis_size("row")),
        "row",
        scatter_dimension=0,
        tiled=True,
    )


def body(
    leaf_rhs,
    sep_rhs,
    top_rhs,
    leaf_inv,
    sep_inv,
    top_inv,
    sep_leaf,
    top_leaf,
    top_sep,
    sep_leaf_mask,
    top_leaf_mask,
    top_sep_mask,
):
    leaf_count = leaf_rhs.shape[2]
    tile_width = leaf_rhs.shape[4]
    rhs_cols = leaf_rhs.shape[5]
    col_count = sep_leaf.shape[2]
    row_count = sep_leaf.shape[4]
    rows_out = col_count * tile_width
    leaf_span = leaf_count * tile_width
    contract = (((0,), (0,)), ((), ()))
    sep_tiles = mask_tiles(sep_leaf[0, 0, :, :, :, :, 0], sep_leaf_mask[0, 0, :, :, :, 0])
    top_tiles = mask_tiles(top_leaf[0, 0, :, :, :, :, 0], top_leaf_mask[0, 0, :, :, :, 0])
    cross_tiles = (
        top_sep[0, 0, :, :, :, 0]
        * top_sep_mask[0, 0, :, :, 0].astype(jnp.bfloat16)[:, None, :, None]
    )
    leaf_y = lower_apply(leaf_inv[0, 0, :, 0], leaf_rhs[0, 0, :, 0].astype(jnp.float32))
    leaf_send = leaf_y.astype(jnp.bfloat16)

    def leaf_update(totals, pieces, offset):
        how_many = pieces.shape[0]
        flat_values = pieces.reshape(how_many * leaf_span, rhs_cols)
        sep_block = sep_tiles.reshape(rows_out, how_many * leaf_span)
        top_block = top_tiles.reshape(rows_out, how_many * leaf_span)
        return (
            jnp.dot(sep_block, flat_values, preferred_element_type=jnp.float32),
            jnp.dot(top_block, flat_values, preferred_element_type=jnp.float32),
        )

    empty_sum = jnp.zeros((rows_out, rhs_cols), jnp.float32)
    sep_part, top_part = spread_down(leaf_send[None], leaf_update, (empty_sum, empty_sum))
    sep_total = reduce_row(sep_part, rhs_cols)
    sep_y = lower_apply(sep_inv[0, 0, 0], sep_rhs[0, 0, 0].astype(jnp.float32) - sep_total)
    sep_send = sep_y.astype(jnp.bfloat16)

    def sep_update(totals, pieces, offset):
        how_many = pieces.shape[0]
        tile_block = cross_tiles.reshape(rows_out, how_many * tile_width)
        return totals + jnp.dot(
            tile_block,
            pieces.reshape(how_many * tile_width, rhs_cols),
            preferred_element_type=jnp.float32,
        )

    top_part = spread_down(sep_send[None], sep_update, top_part)
    top_total = reduce_row(add_sections(top_part), rhs_cols)
    top_y = lower_apply(top_inv[0, 0], top_rhs[0, 0].astype(jnp.float32) - top_total)
    top_x = upper_apply(top_inv[0, 0], top_y)
    top_flat = spread_across(top_x.astype(jnp.bfloat16)).reshape(rows_out, rhs_cols)
    cross_flat = cross_tiles.reshape(rows_out, row_count * tile_width)
    sep_flat_tiles = sep_tiles.reshape(rows_out, row_count * leaf_span)
    top_flat_tiles = top_tiles.reshape(rows_out, row_count * leaf_span)

    def sep_terms(offset, how_many):
        return lax.dot_general(cross_flat, top_flat, contract, preferred_element_type=jnp.float32)

    sep_t = collect_up(sep_terms, tile_width)
    sep_x = upper_apply(sep_inv[0, 0, 0], sep_y - sep_t)
    sep_row = spread_across(sep_x.astype(jnp.bfloat16)).reshape(rows_out, rhs_cols)

    def both_terms(offset, how_many):
        return lax.dot_general(
            sep_flat_tiles, sep_row, contract, preferred_element_type=jnp.float32
        ) + lax.dot_general(top_flat_tiles, top_flat, contract, preferred_element_type=jnp.float32)

    leaf_t = collect_up(both_terms, leaf_span)
    leaf_x = upper_apply(
        leaf_inv[0, 0, :, 0], leaf_y - leaf_t.reshape(leaf_count, tile_width, rhs_cols)
    )
    return (leaf_x[None, None, :, None], sep_x[None, None, None], top_x[None, None])


def solution(mesh):
    in_specs = (
        P("sec", "row", None, "col", None, None),
        P("sec", "row", "col", None, None),
        P("row", "col", None, None),
        P("sec", "row", None, "col", None, None),
        P("sec", "row", "col", None, None),
        P("row", "col", None, None),
        P("sec", "row", None, None, None, None, "col", None),
        P("sec", "row", None, None, None, None, "col", None),
        P("sec", "row", None, None, None, "col", None),
        P("sec", "row", None, None, None, "col"),
        P("sec", "row", None, None, None, "col"),
        P("sec", "row", None, None, "col"),
    )
    out_specs = (
        P("sec", "row", None, "col", None, None),
        P("sec", "row", "col", None, None),
        P("row", "col", None, None),
    )
    return jax.shard_map(body, mesh=mesh, in_specs=in_specs, out_specs=out_specs, check_vma=False)
```

profile of v0, /device:TPU:8, one launch (start us, length us, event | category | flops | bytes accessed | tf_op | source)
XLA Modules:
  0.0 758.6 jit_solution(15964059549455217081)
XLA Ops:
  7.2 1.1 fusion.38
  8.3 12.6 %all-gather = bf16[512,256]{1,0:T(8,128)(2,1)S(1)} all-gather(bf16[128,256]{1,0:T(8,128)(2,1)S(1)} %get-tuple-element.6), channel_id=2, replica_groups=mesh['sec'=2,'row'=4,'col'=32] {'row'}, dimensions={0}, use_global_device_ids=true | all-gather | bytes 327680 | tf_op jit(solution)/shard_map/all_gather | solution.py:20
  21.7 6.0 broadcast_multiply_fusion.2
  27.7 7.2 mul.49
  34.9 5.4 fusion.17
  41.2 4.0 broadcast_multiply_fusion
  45.3 3.3 fusion.5
  50.4 3.8 broadcast_multiply_fusion.1
  54.2 211.2 %reduce-scatter.5.cloned.1.call-done = f32[1,128,256]{2,1,0:T(8,128)} async-done(((f32[32,128,256]{2,1,0:T(8,128)}), f32[1,128,256]{2,1,0:T(8,128)}) %reduce-scatter.5.cloned.1.call-update) | async-done | bytes 131088 | tf_op jit(solution)/shard_map/reduce_scatter | solution.py:25
  265.4 1.3 fusion.39
  266.7 11.9 %all-gather.1 = bf16[512,256]{0,1:T(8,128)(2,1)S(1)} all-gather(bf16[128,256]{0,1:T(8,128)(2,1)S(1)} %get-tuple-element.8), channel_id=3, replica_groups=mesh['sec'=2,'row'=4,'col'=32] {'row'}, dimensions={0}, use_global_device_ids=true | all-gather | bytes 327680 | tf_op jit(solution)/shard_map/all_gather | solution.py:20
  278.6 6.7 convolution_add_fusion
  285.4 220.9 %reduce-scatter.11.cloned.1.call-done = f32[1,128,256]{2,1,0:T(8,128)} async-done(((f32[32,128,256]{2,1,0:T(8,128)}), f32[1,128,256]{2,1,0:T(8,128)}) %reduce-scatter.11.cloned.1.call-update) | async-done | bytes 131088 | tf_op jit(solution)/shard_map/reduce_scatter | solution.py:25
  506.3 30.3 %all-reduce.2.cloned.1.call-done = f32[1,128,256]{2,1,0:T(8,128)} async-done(((f32[1,128,256]{2,1,0:T(8,128)}), f32[1,128,256]{2,1,0:T(8,128)}) %all-reduce.2.cloned.1.call-update) | async-done | bytes 131088 | tf_op jit(solution)/shard_map/psum | solution.py:35
  536.6 1.3 fusion.20
  539.1 76.2 %all-gather.7.cloned.1.call-done = bf16[4096,256]{0,1:T(8,128)(2,1)} async-done(((bf16[128,256]{0,1:T(8,128)(2,1)}), bf16[4096,256]{0,1:T(8,128)(2,1)}) %all-gather.7.cloned.1.call-update) | async-done | bytes 2097168 | tf_op jit(solution)/shard_map/all_gather | solution.py:39
  615.2 5.0 fusion
  620.3 23.6 %reduce-scatter.7.cloned.1.call-done = f32[128,256]{0,1:T(8,128)} async-done(((f32[512,256]{0,1:T(8,128)}), f32[128,256]{0,1:T(8,128)}) %reduce-scatter.7.cloned.1.call-update) | async-done | bytes 131088 | tf_op jit(solution)/shard_map/reduce_scatter | solution.py:43
  643.9 1.8 bitcast_convert_fusion
  645.8 3.5 fusion.3
  649.3 71.8 %all-gather.9.cloned.1.call-done = bf16[4096,256]{0,1:T(8,128)(2,1)} async-done(((bf16[128,256]{0,1:T(8,128)(2,1)}), bf16[4096,256]{0,1:T(8,128)(2,1)}) %all-gather.9.cloned.1.call-update) | async-done | bytes 2097168 | tf_op jit(solution)/shard_map/all_gather | solution.py:39
  721.0 5.0 fusion.14
  727.6 22.1 %reduce-scatter.9.cloned.1.call-done = f32[128,256]{1,0:T(8,128)} async-done(((f32[512,256]{1,0:T(8,128)}), f32[128,256]{1,0:T(8,128)}) %reduce-scatter.9.cloned.1.call-update) | async-done | bytes 131088 | tf_op jit(solution)/shard_map/reduce_scatter | solution.py:43
  749.7 1.3 convolution_bitcast_fusion
  (44 shorter events, 7.2 us)
Async XLA Ops:
  7.2 258.3 %copy-start = (f32[1,1,1,128,128]{4,3,2,1,0:T(8,128)S(1)}, f32[1,1,1,128,128]{4,3,2,1,0:T(8,128)}, u32[]{:S(2)}) copy-start(f32[1,1,1,128,128]{4,3,2,1,0:T(8,128)} %param.16) | copy-start | bytes 196612
  7.2 258.2 %reduce-scatter.5.cloned.1.call-start = ((), (), s32[]{:S(2)}) async-start(), calls=%async_computation.4 | async-start | bytes 4325376 | tf_op jit(solution)/shard_map/reduce_scatter | solution.py:25
  40.3 0.7 copy-start.7
  40.3 0.8 copy-start.8
  40.3 465.9 %reduce-scatter.11.cloned.1.call-start = ((), (), s32[]{:S(2)}) async-start(), calls=%async_computation.9 | async-start | bytes 4325376 | tf_op jit(solution)/shard_map/reduce_scatter | solution.py:25
  45.2 4.1 copy-start.1
  45.3 5.1 copy-start.2
  50.4 215.1 %copy-start.5 = (bf16[1,1,1,128,256]{4,3,2,1,0:T(8,128)(2,1)S(1)}, bf16[1,1,1,128,256]{4,3,2,1,0:T(8,128)(2,1)}, u32[]{:S(2)}) copy-start(bf16[1,1,1,128,256]{4,3,2,1,0:T(8,128)(2,1)} %param.13) | copy-start | bytes 196612
  285.3 251.3 %copy-start.4 = (f32[1,1,128,128]{3,2,1,0:T(8,128)S(1)}, f32[1,1,128,128]{3,2,1,0:T(8,128)}, u32[]{:S(2)}) copy-start(f32[1,1,128,128]{3,2,1,0:T(8,128)} %param.17) | copy-start | bytes 196612
  285.3 251.3 %copy-start.6 = (bf16[1,1,128,256]{3,2,1,0:T(8,128)(2,1)S(1)}, bf16[1,1,128,256]{3,2,1,0:T(8,128)(2,1)}, u32[]{:S(2)}) copy-start(bf16[1,1,128,256]{3,2,1,0:T(8,128)(2,1)} %param.14) | copy-start | bytes 196612
  285.3 251.3 %all-reduce.2.cloned.1.call-start = ((), (), s32[]{:S(2)}) async-start(), calls=%async_computation.10 | async-start | bytes 262144 | tf_op jit(solution)/shard_map/psum | solution.py:35
  506.3 109.0 %all-gather.7.cloned.1.call-start = ((), (), s32[]{:S(2)}) async-start(), calls=%async_computation.7 | async-start | bytes 2162688 | tf_op jit(solution)/shard_map/all_gather | solution.py:39
  538.8 105.1 %reduce-scatter.7.cloned.1.call-start = ((), (), s32[]{:S(2)}) async-start(), calls=%async_computation.5 | async-start | bytes 655360 | tf_op jit(solution)/shard_map/reduce_scatter | solution.py:43
  615.2 30.5 %copy-start.9 = (bf16[4096,256]{0,1:T(8,128)(2,1)S(1)}, bf16[4096,256]{0,1:T(8,128)(2,1)}, u32[]{:S(2)}) copy-start(bf16[4096,256]{0,1:T(8,128)(2,1)} %all-gather.7.cloned.1.call-done) | copy-start | bytes 6291460
  620.3 100.8 %all-gather.9.cloned.1.call-start = ((), (), s32[]{:S(2)}) async-start(), calls=%async_computation.8 | async-start | bytes 2162688 | tf_op jit(solution)/shard_map/all_gather | solution.py:39
  645.7 104.0 %reduce-scatter.9.cloned.1.call-start = ((), (), s32[]{:S(2)}) async-start(), calls=%async_computation.6 | async-start | bytes 655360 | tf_op jit(solution)/shard_map/reduce_scatter | solution.py:43
  721.0 28.7 %copy-start.3 = (f32[1,1,1,1,128,128]{5,4,3,2,1,0:T(8,128)S(1)}, f32[1,1,1,1,128,128]{5,4,3,2,1,0:T(8,128)}, u32[]{:S(2)}) copy-start(f32[1,1,1,1,128,128]{5,4,3,2,1,0:T(8,128)} %param.15) | copy-start | bytes 196612
Sparse Core Ops, SparseCore 0:
  40.4 224.9 reduce-scatter.4
  285.4 220.7 reduce-scatter.10
  508.8 27.7 all-reduce.1
  539.5 75.6 all-gather.6
  620.4 23.4 reduce-scatter.6
  646.8 74.1 all-gather.8
  726.2 23.4 reduce-scatter.8
where the time goes:
time: 759 us
  waiting for transfers between devices  656 us (86%)
  matrix products  36.5 us (5%)
  blocking collectives  24.5 us (3%)
  other arithmetic  14.6 us (2%)
  between operations  14.2 us (2%)
  local copies, waits for them, and re-layouts  12.3 us (2%)
    reduce_scatter x2, waiting for transfers between devices, reduce_row(): lax.psum_scatter(partial_value.reshape(col_count, partial_value.shape[0]...  432 us
    all_gather x2, waiting for transfers between devices, spread_across(): return lax.all_gather(values[None], 'col', axis=0, tiled=True)  148 us
    reduce_scatter x2, waiting for transfers between devices, collect_up(): lax.psum_scatter(term_fn(jnp.int32(0), row_span * lax.axis_size('row')),...  45.7 us
    psum x1, waiting for transfers between devices, add_sections(): return lax.psum(partial_value, 'sec')  30.3 us
    all_gather x2, blocking collectives, spread_down(): lax.all_gather(values, 'row', axis=0, tiled=True)  24.5 us
  transfers between devices with their start and end apart: 7, of which 7 were waited for; matrix products, arithmetic and copies ran while one was open for 2% of the time, Pallas kernels for 0%

commit v1 on v0

--- a/solution.py
+++ b/solution.py
@@ -36,7 +36,9 @@
 
 
 def spread_across(values):
-    return lax.all_gather(values[None], "col", axis=0, tiled=True)
+    return jnp.concatenate(
+        lax.all_to_all(jnp.stack([values[None]] * lax.axis_size("col")), "col", 0, 0), axis=0
+    )
 
 
 def collect_up(term_fn, row_span):

time: 759 us -> 718 us (0.946)
  waiting for transfers between devices: 656 us -> 546 us
  blocking collectives: 24.5 us -> 85.7 us
  starting transfers between devices: 0.47 us -> 10.4 us
    all_gather x2 -> x0, waiting for transfers between devices: 148 us -> none  [spread_across(): return lax.all_gather(values[None], 'col', axis=0, tiled=True)]
    all_to_all x0 -> x1, blocking collectives: none -> 61.2 us  [spread_across(): lax.all_to_all(jnp.stack([values[None]] * lax.axis_size('col')), 'col', 0...]
    all_to_all x0 -> x1, waiting for transfers between devices: none -> 44 us  [spread_across(): lax.all_to_all(jnp.stack([values[None]] * lax.axis_size('col')), 'col', 0...]
    all_to_all x0 -> x1, starting transfers between devices: none -> 10.2 us  [spread_across(): lax.all_to_all(jnp.stack([values[None]] * lax.axis_size('col')), 'col', 0...]
  transfers between devices with their start and end apart: 7 -> 6, of which waited for: 7 -> 6; matrix products, arithmetic and copies ran while one was open for 2% -> 2% of each run, Pallas kernels for 0% -> 0%
where the time goes in v1:
time: 718 us
  waiting for transfers between devices  546 us (76%)
  blocking collectives  85.7 us (12%)
  matrix products  32.3 us (4%)
  other arithmetic  14.6 us (2%)
  local copies, waits for them, and re-layouts  14.3 us (2%)
  between operations  13.9 us (2%)
  starting transfers between devices  10.4 us (1%)
    reduce_scatter x2, waiting for transfers between devices, reduce_row(): lax.psum_scatter(partial_value.reshape(col_count, partial_value.shape[0]...  432 us
    all_to_all x1, blocking collectives, spread_across(): lax.all_to_all(jnp.stack([values[None]] * lax.axis_size('col')), 'col', 0...  61.2 us
    all_to_all x1, waiting for transfers between devices, spread_across(): lax.all_to_all(jnp.stack([values[None]] * lax.axis_size('col')), 'col', 0...  44 us
    reduce_scatter x2, waiting for transfers between devices, collect_up(): lax.psum_scatter(term_fn(jnp.int32(0), row_span * lax.axis_size('row')),...  39.7 us
    psum x1, waiting for transfers between devices, add_sections(): return lax.psum(partial_value, 'sec')  30.4 us
    all_gather x2, blocking collectives, spread_down(): lax.all_gather(values, 'row', axis=0, tiled=True)  24.5 us
  transfers between devices with their start and end apart: 6, of which 6 were waited for; matrix products, arithmetic and copies ran while one was open for 2% of the time, Pallas kernels for 0%

profile of v1, /device:TPU:8, one launch (start us, length us, event | category | flops | bytes accessed | tf_op | source)
XLA Modules:
  0.0 717.5 jit_solution(5074801009649368815)
XLA Ops:
  8.3 12.6 %all-gather = bf16[512,256]{1,0:T(8,128)(2,1)S(1)} all-gather(bf16[128,256]{1,0:T(8,128)(2,1)S(1)} %get-tuple-element.6), channel_id=2, replica_groups=mesh['sec'=2,'row'=4,'col'=32] {'row'}, dimensions={0}, use_global_device_ids=true | all-gather | bytes 327680 | tf_op jit(solution)/shard_map/all_gather | solution.py:20
  21.7 6.0 broadcast_multiply_fusion.2
  27.7 7.3 %mul.49 = bf16[32,128,512]{2,1,0:T(8,128)(2,1)} reshape(bf16[1,1,32,128,4,1,1,128]{7,4,6,5,3,2,1,0:T(4,128)(2,1)} %broadcast_multiply_fusion.2) | data formatting | bytes 8388608 | tf_op jit(solution)/shard_map/mul | solution.py:16
  35.0 5.4 fusion.17
  41.3 4.0 broadcast_multiply_fusion
  45.3 3.3 fusion.2
  50.4 3.8 broadcast_multiply_fusion.1
  54.2 211.3 %reduce-scatter.5.cloned.1.call-done = f32[1,128,256]{2,1,0:T(8,128)} async-done(((f32[32,128,256]{2,1,0:T(8,128)}), f32[1,128,256]{2,1,0:T(8,128)}) %reduce-scatter.5.cloned.1.call-update) | async-done | bytes 131088 | tf_op jit(solution)/shard_map/reduce_scatter | solution.py:25
  265.5 1.3 fusion.39
  266.8 11.9 %all-gather.1 = bf16[512,256]{0,1:T(8,128)(2,1)S(1)} all-gather(bf16[128,256]{0,1:T(8,128)(2,1)S(1)} %get-tuple-element.8), channel_id=3, replica_groups=mesh['sec'=2,'row'=4,'col'=32] {'row'}, dimensions={0}, use_global_device_ids=true | all-gather | bytes 327680 | tf_op jit(solution)/shard_map/all_gather | solution.py:20
  278.7 6.7 convolution_add_fusion
  285.5 220.9 %reduce-scatter.11.cloned.1.call-done = f32[1,128,256]{2,1,0:T(8,128)} async-done(((f32[32,128,256]{2,1,0:T(8,128)}), f32[1,128,256]{2,1,0:T(8,128)}) %reduce-scatter.11.cloned.1.call-update) | async-done | bytes 131088 | tf_op jit(solution)/shard_map/reduce_scatter | solution.py:25
  506.5 30.4 %all-reduce.2.cloned.1.call-done = f32[1,128,256]{2,1,0:T(8,128)} async-done(((f32[1,128,256]{2,1,0:T(8,128)}), f32[1,128,256]{2,1,0:T(8,128)}) %all-reduce.2.cloned.1.call-update) | async-done | bytes 131088 | tf_op jit(solution)/shard_map/psum | solution.py:35
  536.8 1.3 fusion.20
  538.8 61.2 %all_to_all.10 = bf16[32,1,128,256]{3,2,1,0:T(8,128)(2,1)S(1)} all-to-all(bf16[32,1,128,256]{3,2,1,0:T(8,128)(2,1)S(1)} %stack.6), channel_id=1, replica_groups=mesh['sec'=2,'row'=4,'col'=32] {'col'}, dimensions={0} | all-to-all | bytes 4194304 | tf_op jit(solution)/shard_map/all_to_all | solution.py:40
  599.9 2.1 fusion.4
  602.1 21.0 %reduce-scatter.7.cloned.1.call-done = f32[128,256]{0,1:T(8,128)} async-done(((f32[512,256]{0,1:T(8,128)}), f32[128,256]{0,1:T(8,128)}) %reduce-scatter.7.cloned.1.call-update) | async-done | bytes 131088 | tf_op jit(solution)/shard_map/reduce_scatter | solution.py:45
  624.4 1.6 stack.7
  626.0 10.2 %all-to-all-start.1 = ((bf16[32,1,128,256]{3,2,1,0:T(8,128)(2,1)}), bf16[32,1,128,256]{3,2,1,0:T(8,128)(2,1)}, u32[]{:S(2)}, u32[]{:S(2)}) async-start(bf16[32,1,128,256]{3,2,1,0:T(8,128)(2,1)} %stack.7), calls=%async_computation.3 | async-start | bytes 4194304 | tf_op jit(solution)/shard_map/all_to_all | solution.py:40
  636.3 3.5 fusion
  639.8 44.0 %all-to-all-done.1 = bf16[32,1,128,256]{3,2,1,0:T(8,128)(2,1)} async-done(((bf16[32,1,128,256]{3,2,1,0:T(8,128)(2,1)}), bf16[32,1,128,256]{3,2,1,0:T(8,128)(2,1)}, u32[]{:S(2)}, u32[]{:S(2)}) %all-to-all-start.1) | async-done | bytes 2097184 | tf_op jit(solution)/shard_map/all_to_all | solution.py:40
  683.7 5.0 fusion.14
  690.3 18.7 %reduce-scatter.9.cloned.1.call-done = f32[128,256]{1,0:T(8,128)} async-done(((f32[512,256]{1,0:T(8,128)}), f32[128,256]{1,0:T(8,128)}) %reduce-scatter.9.cloned.1.call-update) | async-done | bytes 131088 | tf_op jit(solution)/shard_map/reduce_scatter | solution.py:45
  709.0 1.3 convolution_bitcast_fusion
  (45 shorter events, 9.0 us)
Async XLA Ops:
  7.2 258.3 %copy-start = (f32[1,1,1,128,128]{4,3,2,1,0:T(8,128)S(1)}, f32[1,1,1,128,128]{4,3,2,1,0:T(8,128)}, u32[]{:S(2)}) copy-start(f32[1,1,1,128,128]{4,3,2,1,0:T(8,128)} %param.16) | copy-start | bytes 196612
  7.2 258.3 %reduce-scatter.5.cloned.1.call-start = ((), (), s32[]{:S(2)}) async-start(), calls=%async_computation.6 | async-start | bytes 4325376 | tf_op jit(solution)/shard_map/reduce_scatter | solution.py:25
  40.4 0.7 copy-start.8
  40.4 0.8 copy-start.9
  40.4 466.0 %reduce-scatter.11.cloned.1.call-start = ((), (), s32[]{:S(2)}) async-start(), calls=%async_computation.9 | async-start | bytes 4325376 | tf_op jit(solution)/shard_map/reduce_scatter | solution.py:25
  45.3 4.1 copy-start.2
  45.3 5.1 copy-start.3
  50.4 215.1 %copy-start.6 = (bf16[1,1,1,128,256]{4,3,2,1,0:T(8,128)(2,1)S(1)}, bf16[1,1,1,128,256]{4,3,2,1,0:T(8,128)(2,1)}, u32[]{:S(2)}) copy-start(bf16[1,1,1,128,256]{4,3,2,1,0:T(8,128)(2,1)} %param.13) | copy-start | bytes 196612
  285.4 251.4 %copy-start.5 = (f32[1,1,128,128]{3,2,1,0:T(8,128)S(1)}, f32[1,1,128,128]{3,2,1,0:T(8,128)}, u32[]{:S(2)}) copy-start(f32[1,1,128,128]{3,2,1,0:T(8,128)} %param.17) | copy-start | bytes 196612
  285.4 251.4 %copy-start.7 = (bf16[1,1,128,256]{3,2,1,0:T(8,128)(2,1)S(1)}, bf16[1,1,128,256]{3,2,1,0:T(8,128)(2,1)}, u32[]{:S(2)}) copy-start(bf16[1,1,128,256]{3,2,1,0:T(8,128)(2,1)} %param.14) | copy-start | bytes 196612
  285.4 251.4 %all-reduce.2.cloned.1.call-start = ((), (), s32[]{:S(2)}) async-start(), calls=%async_computation.10 | async-start | bytes 262144 | tf_op jit(solution)/shard_map/psum | solution.py:35
  506.4 116.7 %reduce-scatter.7.cloned.1.call-start = ((), (), s32[]{:S(2)}) async-start(), calls=%async_computation.7 | async-start | bytes 655360 | tf_op jit(solution)/shard_map/reduce_scatter | solution.py:45
  538.5 61.4 %copy-start.1 = (bf16[1,1,32,128,4,1,128]{6,4,5,3,2,1,0:T(4,128)(2,1)S(1)}, bf16[1,1,32,128,4,1,128]{6,4,5,3,2,1,0:T(4,128)(2,1)}, u32[]{:S(2)}) copy-start(bf16[1,1,32,128,4,1,128]{6,4,5,3,2,1,0:T(4,128)(2,1)} %broadcast_multiply_fusion.1) | copy-start | bytes 12582916
  626.0 57.8 %all-to-all-start.1 = ((bf16[32,1,128,256]{3,2,1,0:T(8,128)(2,1)}), bf16[32,1,128,256]{3,2,1,0:T(8,128)(2,1)}, u32[]{:S(2)}, u32[]{:S(2)}) async-start(bf16[32,1,128,256]{3,2,1,0:T(8,128)(2,1)} %stack.7), calls=%async_computation.3 | async-start | bytes 4194304 | tf_op jit(solution)/shard_map/all_to_all | solution.py:40
  636.2 72.7 %reduce-scatter.9.cloned.1.call-start = ((), (), s32[]{:S(2)}) async-start(), calls=%async_computation.8 | async-start | bytes 655360 | tf_op jit(solution)/shard_map/reduce_scatter | solution.py:45
  683.7 25.2 %copy-start.4 = (f32[1,1,1,1,128,128]{5,4,3,2,1,0:T(8,128)S(1)}, f32[1,1,1,1,128,128]{5,4,3,2,1,0:T(8,128)}, u32[]{:S(2)}) copy-start(f32[1,1,1,1,128,128]{5,4,3,2,1,0:T(8,128)} %param.15) | copy-start | bytes 196612
Sparse Core Ops, SparseCore 0:
  40.5 224.9 reduce-scatter.4
  285.5 220.7 reduce-scatter.10
  508.9 27.8 all-reduce.1
  602.2 20.8 reduce-scatter.6
  688.9 20.0 reduce-scatter.8
